TPU v7x, 32 devices: a whole 2x2x4 slice. The times are simulated.
32 devices in a mesh: series: 4 (over y, x), tm: 8 (over z, core).
Axes of the slice: x: 2, y: 2, z: 4, core: 2. Of those that a mesh axis runs over, the one named last changes fastest.
Arguments:
- observed: bfloat16 [5120, 6144], P('series', 'tm'), may hold values from -6 to 6
- mask: int32 [5120, 6144], P('series', 'tm'), may hold values 0 or 1
- series_factors: float32 [5120, 256], P('series'), may hold values from -6 to 6
- time_factors: float32 [256, 6144], P(None, 'tm'), may hold values from -0.375 to 0.375
- ar_weights: float32 [3, 256], replicated, may hold values from -0.7 to 0.7
Outputs:
- series_out: float32 [5120, 256], P('series')
- time_out: float32 [256, 6144], P(None, 'tm')
- imputed: bfloat16 [5120, 6144], P('series', 'tm')
Inputs may be any that keep to these rules, and one draw needn't show every extreme that they name: mask holds only 0 and 1.
All inputs are finite; a program needn't handle non-finite values. No bound on the sum of `mask` on one device may be relied on, other than what follows from the above.
Results may differ from a plain program's by a relative error of at most 0.0089.
Values sent between devices are 32-bit elements; how exact they have to be, the bound alone decides.
A program may use at most 128 MiB of HBM per device.

v0:
```python
import jax
import jax.numpy as jnp
from jax import lax
from jax.sharding import PartitionSpec as P

ITERS = 2


lag_hours = (1, 24, 168)


def passed_along(array, axis, by):
    length = lax.axis_size(axis)
    pairs = [(i, i + by) for i in range(length) if 0 <= i + by < length]
    return lax.ppermute(array, axis, pairs)


def combine_lags(extended, weights, offset, width):
    total = None
    for lag_index, lag_size in enumerate(lag_hours):
        begin = offset + lag_size
        piece = weights[lag_index][:, None] * extended[:, begin : begin + width]
        total = piece if total is None else total + piece
    return total


def local(observed, mask, series_factors, time_factors, ar_weights):
    row_count, hour_count = observed.shape
    factor_rank = time_factors.shape[0]
    hours_all = hour_count * lax.axis_size("tm")
    sensors_all = row_count * lax.axis_size("series")
    step_f = factor_rank / hours_all
    step_x = 1.0 / sensors_all
    ridge_f = 0.1 * hours_all / factor_rank
    ridge_x = 0.1 * sensors_all
    lam_ar = sensors_all / 8.0
    first_hour = lax.axis_index("tm") * hour_count
    share_rows = row_count // lax.axis_size("tm")
    series_now = series_factors
    time_now = time_factors
    for sweep in range(ITERS):
        series_low = series_now.astype(jnp.bfloat16)
        time_low = time_now.astype(jnp.bfloat16)
        product = jnp.dot(series_low, time_low, preferred_element_type=jnp.float32)
        misfit = jnp.where(
            mask != 0, product - observed.astype(jnp.float32), jnp.zeros_like(product)
        ).astype(jnp.bfloat16)
        grad_share = lax.psum_scatter(
            lax.dot_general(
                misfit, time_low, (((1,), (1,)), ((), ())), preferred_element_type=jnp.float32
            ),
            "tm",
            scatter_dimension=0,
            tiled=True,
        )
        own_rows = lax.dynamic_slice_in_dim(
            series_now, lax.axis_index("tm") * share_rows, share_rows, 0
        )
        updated = own_rows - step_f * (grad_share + ridge_f * own_rows)
        series_next = lax.all_gather(updated, "tm", axis=0, tiled=True)
        grad_data = lax.psum(
            lax.dot_general(
                series_low, misfit, (((0,), (0,)), ((), ())), preferred_element_type=jnp.float32
            ),
            "series",
        )
        left_edge = passed_along(time_now[:, hour_count - 168 :], "tm", 1)
        extended = jnp.concatenate([left_edge, time_now], axis=1)
        lag_resid = time_now
        for lag_index, lag_size in enumerate(lag_hours):
            lag_resid = (
                lag_resid
                - ar_weights[lag_index][:, None]
                * extended[:, 168 - lag_size : 168 - lag_size + hour_count]
            )
        in_range = first_hour + jnp.arange(hour_count) >= 168
        lag_resid = jnp.where(in_range[None, :], lag_resid, jnp.zeros_like(lag_resid))
        right_edge = passed_along(lag_resid[:, :168], "tm", -1)
        resid_wide = jnp.concatenate([lag_resid, right_edge], axis=1)
        backward = combine_lags(resid_wide, ar_weights, 0, hour_count)
        time_next = time_now - step_x * (
            grad_data + ridge_x * time_now + lam_ar * (lag_resid - backward)
        )
        series_now, time_now = (series_next, time_next)
    imputed = jnp.dot(
        series_now.astype(jnp.bfloat16),
        time_now.astype(jnp.bfloat16),
        preferred_element_type=jnp.float32,
    ).astype(jnp.bfloat16)
    return (series_now, time_now, imputed)


def solution(mesh):
    in_specs = (P("series", "tm"), P("series", "tm"), P("series", None), P(None, "tm"), P())
    out_specs = (P("series", None), P(None, "tm"), P("series", "tm"))
    return jax.shard_map(local, mesh=mesh, in_specs=in_specs, out_specs=out_specs, check_vma=False)
```

profile of v0, /device:TPU:0, one launch (start us, length us, event | category | flops | bytes accessed | tf_op | source)
XLA Modules:
  0.0 150.2 jit_solution(12942424839091787382)
XLA Ops:
  8.1 2.8 %broadcast_compare_fusion = pred[1280,768]{1,0:T(32,128)(4,1)S(1)} fusion(s32[1280,768]{1,0:T(8,128)} %param.6), kind=kLoop, calls=%fused_computation.7 | loop fusion | flops 983040 | bytes 4915200 | tf_op jit(solution)/shard_map/ne | solution.py:46
  12.3 1.8 %fusion.56 = f32[1280,256]{1,0:T(8,128)} fusion(bf16[1280,768]{1,0:T(8,128)(2,1)S(1)} %fusion.2, f32[256,768]{1,0:T(8,128)S(1)} %copy-done.2), kind=kOutput, calls=%fused_computation.81 | convolution fusion | flops 503513088 | bytes 4063232 | tf_op jit(solution)/shard_map/dot_general | solution.py:49
  14.1 2.9 %convolution_bitcast_fusion = f32[256,768]{0,1:T(8,128)} fusion(bf16[1280,768]{1,0:T(8,128)(2,1)S(1)} %fusion.2, f32[1280,256]{1,0:T(8,128)} %param.7), kind=kOutput, calls=%fused_computation.8 | convolution fusion | flops 503644160 | bytes 4063232 | tf_op jit(solution)/shard_map/dot_general | solution.py:62
  17.1 33.0 %reduce-scatter.3.cloned.1.call-done = f32[160,256]{1,0:T(8,128)} async-done(((f32[1280,256]{1,0:T(8,128)}), f32[160,256]{1,0:T(8,128)}) %reduce-scatter.3.cloned.1.call-update) | async-done | bytes 163856 | tf_op jit(solution)/shard_map/reduce_scatter | solution.py:48
  50.2 1.7 %multiply_subtract_fusion.1 = f32[160,256]{1,0:T(8,128)} fusion(f32[160,256]{1,0:T(8,128)} %reduce-scatter.3.cloned.1.call-done, f32[1280,256]{1,0:T(8,128)} %param.7, s32[]{:T(128)S(6)} %select_n.18), kind=kLoop, calls=%fused_computation.85 | loop fusion | flops 163840 | bytes 491524 | tf_op jit(solution)/shard_map/sub | solution.py:59
  52.3 1.3 collective-permute-start
  54.9 1.3 collective-permute-start.1
  56.2 2.0 %collective-permute-done.1 = f32[256,168]{0,1:T(8,128)S(1)} collective-permute-done((f32[256,168]{0,1:T(8,128)S(1)}, f32[256,168]{0,1:T(8,128)S(1)}, u32[]{:S(2)}, u32[]{:S(2)}) %collective-permute-start.1) | collective-permute-done | bytes 172064 | tf_op jit(solution)/shard_map/ppermute | solution.py:15
  58.2 10.9 %all-reduce.3.cloned.1.call-done = f32[256,768]{0,1:T(8,128)} async-done(((f32[256,768]{0,1:T(8,128)}), f32[256,768]{0,1:T(8,128)}) %all-reduce.3.cloned.1.call-update) | async-done | bytes 786448 | tf_op jit(solution)/shard_map/psum | solution.py:61
  69.1 1.5 %fusion.31 = f32[256,768]{0,1:T(8,128)S(1)} fusion(f32[256,768]{0,1:T(8,128)S(1)} %copy.12, f32[256,768]{0,1:T(8,128)S(1)} %fusion.38, f32[256,168]{0,1:T(8,128)S(1)} %collective-permute-done.1, f32[256,768]{0,1:T(8,128)} %all-reduce.3.cloned.1.call-done, f32[256]{0:T(256)S(1)} %bitcast.14, f32[256]{0:T(256)S(1)} %bitcast.18, f32[256]{0:T(256)S(1)} %bitcast.10), kind=kLoop, calls=%fused_computation.52 | loop fusion | flops 2949120 | bytes 3320832 | tf_op jit(solution)/shard_map/sub | solution.py:81
  70.6 5.2 %all-gather.3.cloned.1.call-done = f32[1280,256]{1,0:T(8,128)} async-done(((f32[160,256]{1,0:T(8,128)}), f32[1280,256]{1,0:T(8,128)}) %all-gather.3.cloned.1.call-update) | async-done | bytes 1310736 | tf_op jit(solution)/shard_map/all_gather | solution.py:60
  75.8 3.2 %fusion.3 = bf16[1280,768]{1,0:T(8,128)(2,1)S(1)} fusion(pred[1280,768]{1,0:T(32,128)(4,1)} %copy-done, bf16[1280,768]{1,0:T(8,128)(2,1)} %param.5, f32[1280,256]{1,0:T(8,128)} %all-gather.3.cloned.1.call-done, f32[256,768]{0,1:T(8,128)S(1)} %fusion.31), kind=kOutput, calls=%fused_computation.6 | convolution fusion | flops 507772928 | bytes 7012352 | tf_op jit(solution)/shard_map/dot_general | solution.py:44
  79.0 1.7 %fusion.53 = f32[1280,256]{1,0:T(8,128)} fusion(bf16[1280,768]{1,0:T(8,128)(2,1)S(1)} %fusion.3, f32[256,768]{0,1:T(8,128)S(1)} %fusion.31), kind=kOutput, calls=%fused_computation.78 | convolution fusion | flops 503513088 | bytes 4063232 | tf_op jit(solution)/shard_map/dot_general | solution.py:49
  80.8 3.1 %fusion.48 = f32[256,768]{0,1:T(8,128)} fusion(bf16[1280,768]{1,0:T(8,128)(2,1)S(1)} %fusion.3, f32[1280,256]{1,0:T(8,128)} %all-gather.3.cloned.1.call-done), kind=kOutput, calls=%fused_computation.73 | convolution fusion | flops 503644160 | bytes 4063232 | tf_op jit(solution)/shard_map/dot_general | solution.py:62
  84.0 29.5 %reduce-scatter.5.cloned.1.call-done = f32[160,256]{1,0:T(8,128)} async-done(((f32[1280,256]{1,0:T(8,128)}), f32[160,256]{1,0:T(8,128)}) %reduce-scatter.5.cloned.1.call-update) | async-done | bytes 163856 | tf_op jit(solution)/shard_map/reduce_scatter | solution.py:48
  113.5 1.7 %multiply_subtract_fusion = f32[160,256]{1,0:T(8,128)} fusion(f32[160,256]{1,0:T(8,128)} %reduce-scatter.5.cloned.1.call-done, f32[1280,256]{1,0:T(8,128)} %all-gather.3.cloned.1.call-done, s32[]{:T(128)S(6)} %select_n.18), kind=kLoop, calls=%fused_computation.84 | loop fusion | flops 163840 | bytes 491524 | tf_op jit(solution)/shard_map/sub | solution.py:59
  115.2 1.3 collective-permute-start.2
  117.8 1.3 collective-permute-start.3
  119.1 2.0 %collective-permute-done.3 = f32[256,168]{0,1:T(8,128)S(1)} collective-permute-done((f32[256,168]{0,1:T(8,128)S(1)}, f32[256,168]{0,1:T(8,128)S(1)}, u32[]{:S(2)}, u32[]{:S(2)}) %collective-permute-start.3) | collective-permute-done | bytes 172064 | tf_op jit(solution)/shard_map/ppermute | solution.py:15
  121.1 11.2 %all-reduce.5.cloned.1.call-done = f32[256,768]{0,1:T(8,128)} async-done(((f32[256,768]{0,1:T(8,128)}), f32[256,768]{0,1:T(8,128)}) %all-reduce.5.cloned.1.call-update) | async-done | bytes 786448 | tf_op jit(solution)/shard_map/psum | solution.py:61
  132.3 1.5 fusion.12
  133.8 1.1 copy.14
  134.9 3.7 %all-gather.5.cloned.1.call-done = f32[1280,256]{1,0:T(8,128)} async-done(((f32[160,256]{1,0:T(8,128)}), f32[1280,256]{1,0:T(8,128)}) %all-gather.5.cloned.1.call-update) | async-done | bytes 1310736 | tf_op jit(solution)/shard_map/all_gather | solution.py:60
  138.6 3.4 %convolution_convert_fusion = bf16[1280,768]{1,0:T(8,128)(2,1)} fusion(f32[1280,256]{1,0:T(8,128)} %all-gather.5.cloned.1.call-done, f32[256,768]{0,1:T(8,128)S(1)} %fusion.12), kind=kOutput, calls=%fused_computation.4 | convolution fusion | flops 504823808 | bytes 4063232 | tf_op jit(solution)/shard_map/dot_general | solution.py:85
  (37 shorter events, 5.7 us)
Async XLA Ops:
  8.0 2.9 %copy-start.2 = (f32[256,768]{1,0:T(8,128)S(1)}, f32[256,768]{1,0:T(8,128)}, u32[]{:S(2)}) copy-start(f32[256,768]{1,0:T(8,128)} %param.8) | copy-start | bytes 2359300
  8.0 42.2 %reduce-scatter.3.cloned.1.call-start = ((), (), s32[]{:S(2)}) async-start(), calls=%async_computation.2 | async-start | bytes 1474560 | tf_op jit(solution)/shard_map/reduce_scatter | solution.py:48
  8.1 2.9 %copy-start.1 = (bf16[1280,768]{1,0:T(8,128)(2,1)S(1)}, bf16[1280,768]{1,0:T(8,128)(2,1)}, u32[]{:S(2)}) copy-start(bf16[1280,768]{1,0:T(8,128)(2,1)} %param.5) | copy-start | bytes 5898244
  8.1 3.3 %copy-start.4 = (f32[1280,256]{1,0:T(8,128)S(1)}, f32[1280,256]{1,0:T(8,128)}, u32[]{:S(2)}) copy-start(f32[1280,256]{1,0:T(8,128)} %param.7) | copy-start | bytes 3932164
  11.3 0.9 copy-start
  14.1 55.0 %all-reduce.3.cloned.1.call-start = ((), (), s32[]{:S(2)}) async-start(), calls=%async_computation.4 | async-start | bytes 1572864 | tf_op jit(solution)/shard_map/psum | solution.py:61
  17.1 36.5 %copy-start.5 = (f32[3,256]{1,0:T(4,128)S(1)}, f32[3,256]{1,0:T(4,128)}, u32[]{:S(2)}) copy-start(f32[3,256]{1,0:T(4,128)} %param.9) | copy-start | bytes 9220
  17.1 58.8 %all-gather.3.cloned.1.call-start = ((), (), s32[]{:S(2)}) async-start(), calls=%async_computation.3 | async-start | bytes 1474560 | tf_op jit(solution)/shard_map/all_gather | solution.py:60
  51.9 61.6 %reduce-scatter.5.cloned.1.call-start = ((), (), s32[]{:S(2)}) async-start(), calls=%async_computation.5 | async-start | bytes 1474560 | tf_op jit(solution)/shard_map/reduce_scatter | solution.py:48
  52.3 2.3 %collective-permute-start = (f32[256,168]{0,1:T(8,128)S(1)}, f32[256,168]{0,1:T(8,128)S(1)}, u32[]{:S(2)}, u32[]{:S(2)}) collective-permute-start(f32[256,168]{0,1:T(8,128)S(1)} %slice.85), channel_id=1, source_target_pairs={{0,1},{1,2},{2,3},{3,4},{4,5},{5,6},{6,7},{8,9},{9,10},{10,11},{11... | collective-permute-start | bytes 516104 | tf_op jit(solution)/shard_map/ppermute | solution.py:15
  54.9 3.3 %collective-permute-start.1 = (f32[256,168]{0,1:T(8,128)S(1)}, f32[256,168]{0,1:T(8,128)S(1)}, u32[]{:S(2)}, u32[]{:S(2)}) collective-permute-start(f32[256,168]{0,1:T(8,128)S(1)} %slice.90), channel_id=1, source_target_pairs={{1,0},{2,1},{3,2},{4,3},{5,4},{6,5},{7,6},{9,8},{10,9},{11,10},{12... | collective-permute-start | bytes 516104 | tf_op jit(solution)/shard_map/ppermute | solution.py:15
  80.8 51.5 %all-reduce.5.cloned.1.call-start = ((), (), s32[]{:S(2)}) async-start(), calls=%async_computation.7 | async-start | bytes 1572864 | tf_op jit(solution)/shard_map/psum | solution.py:61
  83.9 54.7 %all-gather.5.cloned.1.call-start = ((), (), s32[]{:S(2)}) async-start(), calls=%async_computation.6 | async-start | bytes 1474560 | tf_op jit(solution)/shard_map/all_gather | solution.py:60
  115.2 2.3 %collective-permute-start.2 = (f32[256,168]{0,1:T(8,128)S(1)}, f32[256,168]{0,1:T(8,128)S(1)}, u32[]{:S(2)}, u32[]{:S(2)}) collective-permute-start(f32[256,168]{0,1:T(8,128)S(1)} %slice.95), channel_id=1, source_target_pairs={{0,1},{1,2},{2,3},{3,4},{4,5},{5,6},{6,7},{8,9},{9,10},{10,11},{11... | collective-permute-start | bytes 516104 | tf_op jit(solution)/shard_map/ppermute | solution.py:15
  117.8 3.3 %collective-permute-start.3 = (f32[256,168]{0,1:T(8,128)S(1)}, f32[256,168]{0,1:T(8,128)S(1)}, u32[]{:S(2)}, u32[]{:S(2)}) collective-permute-start(f32[256,168]{0,1:T(8,128)S(1)} %slice.100), channel_id=1, source_target_pairs={{1,0},{2,1},{3,2},{4,3},{5,4},{6,5},{7,6},{9,8},{10,9},{11,10},{12... | collective-permute-start | bytes 516104 | tf_op jit(solution)/shard_map/ppermute | solution.py:15
  138.6 3.4 %copy-start.3 = (f32[1280,256]{1,0:T(8,128)S(1)}, f32[1280,256]{1,0:T(8,128)}, u32[]{:S(2)}) copy-start(f32[1280,256]{1,0:T(8,128)} %all-gather.5.cloned.1.call-done) | copy-start | bytes 3932164
Sparse Core Ops, SparseCore 0:
  14.2 35.9 reduce-scatter.2
  52.4 23.3 all-gather.2
  80.9 32.5 reduce-scatter.4
  115.5 23.0 all-gather.4
Sparse Core Ops, SparseCore 1:
  18.2 50.9 all-reduce.2
  84.9 47.3 all-reduce.4
where the time goes:
time: 151 us; the launch traced here: 150 us
  waiting for transfers between devices  99.6 us (66%)
  matrix products  17 us (11%)
  between operations  15.4 us (10%)
  other arithmetic  9.74 us (6%)
  starting transfers between devices  5.43 us (4%)
  local copies, waits for them, and re-layouts  3.04 us (2%)
    reduce_scatter x2, waiting for transfers between devices, local(): lax.psum_scatter(lax.dot_general(misfit, time_low, (((1,), (1,)), ((), ()...  62.5 us
    psum x2, waiting for transfers between devices, local(): lax.psum(lax.dot_general(series_low, misfit, (((0,), (0,)), ((), ())), pr...  22.1 us
    all_gather x2, waiting for transfers between devices, local(): series_next = lax.all_gather(updated, 'tm', axis=0, tiled=True)  8.86 us
    dot_general x2, matrix products, local(): lax.dot_general(series_low, misfit, (((0,), (0,)), ((), ())), preferred_e...  6.01 us
    ppermute x4, waiting for transfers between devices, passed_along(): return lax.ppermute(array, axis, pairs)  5.98 us
    ppermute x4, starting transfers between devices, passed_along(): return lax.ppermute(array, axis, pairs)  5.18 us
    dot_general x2, matrix products, local(): product = jnp.dot(series_low, time_low, preferred_element_type=jnp.float32)  4.09 us
    dot_general x2, matrix products, local(): lax.dot_general(misfit, time_low, (((1,), (1,)), ((), ())), preferred_ele...  3.51 us
  transfers between devices with their start and end apart: 10, of which 10 were waited for; matrix products, arithmetic and copies ran while one was open for 10% of the time, Pallas kernels for 0%

commit v1 on v0

v1 whole, which is shorter than its diff:
```python
import functools

import jax
import jax.numpy as jnp
from jax import lax
from jax.experimental import pallas as pl
from jax.experimental.pallas import tpu as pltpu
from jax.sharding import PartitionSpec as P

ITERS = 2
LAGS = (1, 24, 168)
HALO = 256
HALF = 64
BLOCK = 2 * HALF
LAG_STEPS = 4
G_STEP = 8


def kernel(
    series_size, tm_size,
    obs_hbm, mask_hbm, f_in, x_in, w_in,
    f_out, x_out,
    obs, mask, f_new, x_new, misfit, f_low, x_low, grad, partner_in, left_in, right_in,
    g_loc, g_in, halo_l, halo_r, w_cols,
    load_sem, out_sem, pair_send, pair_recv, line_send, left_recv, right_recv,
    out_send, gather_recv, give_send, give_recv, g_send, g_recv, x_send, x_recv,
    edge_send, edge_recv,
):
    rows, rank = f_in.shape
    hours = x_in.shape[1]
    blocks = rows // BLOCK
    piece = rank // series_size
    hours_all = hours * tm_size
    sensors_all = rows * series_size
    step_f = rank / hours_all
    step_x = 1.0 / sensors_all
    ridge_f = 0.1 * hours_all / rank
    ridge_x = 0.1 * sensors_all
    lam_ar = sensors_all / 8.0

    s = lax.axis_index("series")
    tm = lax.axis_index("tm")
    chips = tm_size // 2
    chip, core = tm // 2, tm % 2
    other = 1 - core
    owner = chips // 2 - 1 + core
    partner = chip * 2 + other
    is_owner = chip == owner
    before = chip < owner
    after = chip > owner
    has_left = chip > 0
    has_right = chip < chips - 1
    at_end = jnp.logical_or(jnp.logical_and(before, chip == 0), jnp.logical_and(after, chip == chips - 1))
    relay = jnp.logical_and(jnp.logical_not(is_owner), jnp.logical_not(at_end))

    def both(a, b):
        return jnp.logical_and(a, b)

    def remote(src, dst, ssem, rsem, series_to, tm_to):
        return pltpu.make_async_remote_copy(
            src_ref=src, dst_ref=dst, send_sem=ssem, recv_sem=rsem,
            device_id=(series_to, tm_to), device_id_type=pl.DeviceIdType.MESH,
        )

    def block_rows(b):
        return pl.ds(pl.multiple_of(b * BLOCK, BLOCK), BLOCK)

    def half_rows(b, which):
        return pl.ds(pl.multiple_of(b * BLOCK + which * HALF, HALF), HALF)

    def slot_rows(b):
        return pl.ds(pl.multiple_of(b * HALF, HALF), HALF)

    def piece_rows(i):
        return pl.ds(pl.multiple_of(i * piece, piece), piece)

    def load_copies(b):
        return (
            pltpu.make_async_copy(obs_hbm.at[block_rows(b), :], obs.at[block_rows(b), :], load_sem.at[0, b]),
            pltpu.make_async_copy(mask_hbm.at[block_rows(b), :], mask.at[block_rows(b), :], load_sem.at[1, b]),
        )

    @pl.loop(0, blocks)
    def _(b):
        for c in load_copies(b):
            c.start()

    barrier = pltpu.get_barrier_semaphore()
    for d in (-2, -1, 1, 2):
        @pl.when(both(tm + d >= 0, tm + d < tm_size))
        def _():
            pl.semaphore_signal(barrier, inc=1, device_id=(s, tm + d), device_id_type=pl.DeviceIdType.MESH)
    for d in range(1, series_size):
        pl.semaphore_signal(
            barrier, inc=1, device_id=(lax.rem(s + d, series_size), tm), device_id_type=pl.DeviceIdType.MESH
        )
    pl.semaphore_wait(barrier, series_size - 1 + jnp.minimum(tm, 2) + jnp.minimum(tm_size - 1 - tm, 2))

    def edge_copies(it, source):
        to_right = remote(
            source.at[piece_rows(s), pl.ds(hours - HALO, HALO)], halo_l.at[it],
            edge_send.at[it, 0], edge_recv.at[it, 0], s, tm + 1,
        )
        to_left = remote(
            source.at[piece_rows(s), pl.ds(0, HALO)], halo_r.at[it],
            edge_send.at[it, 1], edge_recv.at[it, 1], s, tm - 1,
        )
        return to_right, to_left

    def start_edges(it, source):
        to_right, to_left = edge_copies(it, source)
        pl.when(tm < tm_size - 1)(to_right.start)
        pl.when(tm > 0)(to_left.start)

    start_edges(0, x_in)
    for lag in range(3):
        w_cols[lag] = jnp.transpose(jnp.broadcast_to(w_in[lag : lag + 1, :], (128, rank)))

    for it in range(ITERS):
        f_now = f_in if it == 0 else f_new.at[it - 1]
        x_now = x_in if it == 0 else x_new.at[it - 1]

        def pair_copy(b, it=it):
            return remote(
                grad.at[it, half_rows(b, other), :], partner_in.at[it, slot_rows(b), :],
                pair_send.at[it, b], pair_recv.at[it, b], s, partner,
            )

        def to_right_copy(b, it=it):
            return remote(
                grad.at[it, half_rows(b, core), :], left_in.at[it, slot_rows(b), :],
                line_send.at[it, b], left_recv.at[it, b], s, tm + 2,
            )

        def to_left_copy(b, it=it):
            return remote(
                grad.at[it, half_rows(b, core), :], right_in.at[it, slot_rows(b), :],
                line_send.at[it, b], right_recv.at[it, b], s, tm - 2,
            )

        def spread_copies(b, it=it):
            rows_own = half_rows(b, core)
            view = f_new.at[it, rows_own, :]
            left = remote(view, view, out_send.at[it, 0, b], gather_recv.at[it, b], s, tm - 2)
            right = remote(view, view, out_send.at[it, 1, b], gather_recv.at[it, b], s, tm + 2)
            give = remote(view, view, give_send.at[it, b], give_recv.at[it, b], s, partner)
            return left, right, give

        def give_wait(b, it=it):
            view = f_new.at[it, half_rows(b, other), :]
            remote(view, view, give_send.at[it, b], give_recv.at[it, b], s, partner).wait_recv()

        def send_inward(b):
            pl.when(before)(to_right_copy(b).start)
            pl.when(after)(to_left_copy(b).start)

        def merge(b):
            pair_copy(b).wait_recv()
            grad[it, half_rows(b, core), :] += partner_in[it, slot_rows(b), :]
            pl.when(at_end)(lambda: send_inward(b))

        x_low[...] = x_now[...].astype(jnp.bfloat16)

        def compute(b, carry):
            if it == 0:
                for c in load_copies(b):
                    c.wait()
            else:
                give_wait(b, it - 1)
            low = f_now[block_rows(b), :].astype(jnp.bfloat16)
            f_low[block_rows(b), :] = low
            product = jnp.dot(low, x_low[...], preferred_element_type=jnp.float32)
            miss = jnp.where(
                mask[block_rows(b), :] != 0,
                product - obs[block_rows(b), :].astype(jnp.float32),
                jnp.zeros_like(product),
            ).astype(jnp.bfloat16)
            misfit[block_rows(b), :] = miss
            grad[it, block_rows(b), :] = lax.dot_general(
                miss, x_low[...], (((1,), (1,)), ((), ())), preferred_element_type=jnp.float32
            )
            pair_copy(b).start()
            pl.when(b > 0)(lambda: merge(b - 1))
            return carry

        lax.fori_loop(0, blocks, compute, 0)
        merge(blocks - 1)

        g_loc[it] = lax.dot_general(
            f_low[...], misfit[...], (((0,), (0,)), ((), ())), preferred_element_type=jnp.float32
        )

        def g_copy(d, it=it):
            to = lax.rem(s + d, series_size)
            return remote(
                g_loc.at[it, piece_rows(to), :], g_in.at[it, d - 1],
                g_send.at[it, d - 1], g_recv.at[it, d - 1], to, tm,
            )

        def x_copy(d, it=it):
            to = lax.rem(s + d, series_size)
            view = x_new.at[it, piece_rows(s), :]
            return remote(view, view, x_send.at[it, d - 1], x_recv.at[it, d - 1], to, tm)

        def x_wait(d, it=it):
            source = lax.rem(s + series_size - d, series_size)
            view = x_new.at[it, piece_rows(source), :]
            remote(view, view, x_send.at[it, d - 1], x_recv.at[it, d - 1], s, tm).wait_recv()

        for d in range(1, series_size):
            g_copy(d).start()

        def relay_step(b):
            @pl.when(both(relay, before))
            def _():
                to_right_copy(b).wait_recv()
                grad[it, half_rows(b, core), :] += left_in[it, slot_rows(b), :]
                to_right_copy(b).start()

            @pl.when(both(relay, after))
            def _():
                to_left_copy(b).wait_recv()
                grad[it, half_rows(b, core), :] += right_in[it, slot_rows(b), :]
                to_left_copy(b).start()

            @pl.when(is_owner)
            def _():
                @pl.when(has_left)
                def _():
                    to_right_copy(b).wait_recv()
                    grad[it, half_rows(b, core), :] += left_in[it, slot_rows(b), :]

                @pl.when(has_right)
                def _():
                    to_left_copy(b).wait_recv()
                    grad[it, half_rows(b, core), :] += right_in[it, slot_rows(b), :]

                old = f_now[half_rows(b, core), :]
                f_new[it, half_rows(b, core), :] = old - step_f * (grad[it, half_rows(b, core), :] + ridge_f * old)
                left, right, give = spread_copies(b)
                pl.when(has_left)(left.start)
                pl.when(has_right)(right.start)
                give.start()

        def spread_step(b):
            left, right, give = spread_copies(b)

            @pl.when(jnp.logical_not(is_owner))
            def _():
                left.wait_recv()
                pl.when(both(before, has_left))(left.start)
                pl.when(both(after, has_right))(right.start)
                give.start()

        def line_step(j, carry):
            pl.when(j < blocks)(lambda: relay_step(j))
            pl.when(j >= LAG_STEPS)(lambda: spread_step(j - LAG_STEPS))
            return carry

        lax.fori_loop(0, G_STEP, line_step, 0)

        to_right, to_left = edge_copies(it, x_now)

        @pl.when(tm > 0)
        def _():
            to_right.wait_recv()

        @pl.when(tm == 0)
        def _():
            halo_l[it] = jnp.zeros_like(halo_l[it])

        @pl.when(tm < tm_size - 1)
        def _():
            to_left.wait_recv()

        @pl.when(tm == tm_size - 1)
        def _():
            halo_r[it] = jnp.zeros_like(halo_r[it])

        own = x_now[piece_rows(s), :]
        extended = jnp.concatenate([halo_l[it], own, halo_r[it]], axis=1)
        width = hours + 2 * HALO
        weights = [w_cols[lag, piece_rows(s), :][:, 0:1] for lag in range(3)]
        resid = extended
        for lag in range(3):
            resid = resid - weights[lag] * pltpu.roll(extended, LAGS[lag], 1)
        hour = lax.broadcasted_iota(jnp.int32, (piece, width), 1) + (tm * hours - HALO)
        resid = jnp.where(both(hour >= 168, hour < hours_all), resid, jnp.zeros_like(resid))
        back = None
        for lag in range(3):
            term = weights[lag] * pltpu.roll(resid, width - LAGS[lag], 1)
            back = term if back is None else back + term
        ar = (resid - back)[:, HALO : HALO + hours]

        total = g_loc[it, piece_rows(s), :]
        for d in range(1, series_size):
            g_copy(d).wait_recv()
            total = total + g_in[it, d - 1]
        x_new[it, piece_rows(s), :] = own - step_x * (total + ridge_x * own + lam_ar * ar)
        for d in range(1, series_size):
            x_copy(d).start()
        if it < ITERS - 1:
            start_edges(it + 1, x_new.at[it])

        lax.fori_loop(G_STEP, blocks + LAG_STEPS, line_step, 0)
        for d in range(1, series_size):
            x_wait(d)

    last = ITERS - 1

    def f_store(b):
        return pltpu.make_async_copy(f_new.at[last, block_rows(b), :], f_out.at[block_rows(b), :], out_sem.at[b])

    x_store = pltpu.make_async_copy(x_new.at[last], x_out, out_sem.at[blocks])
    x_store.start()

    @pl.loop(0, blocks)
    def _(b):
        give_wait(b, last)
        f_store(b).start()

    for it in range(ITERS):
        to_right, to_left = edge_copies(it, x_in if it == 0 else x_new.at[it - 1])
        pl.when(tm < tm_size - 1)(to_right.wait_send)
        pl.when(tm > 0)(to_left.wait_send)
        for d in range(1, series_size):
            to = lax.rem(s + d, series_size)
            remote(
                g_loc.at[it, piece_rows(to), :], g_in.at[it, d - 1],
                g_send.at[it, d - 1], g_recv.at[it, d - 1], to, tm,
            ).wait_send()
            view = x_new.at[it, piece_rows(s), :]
            remote(view, view, x_send.at[it, d - 1], x_recv.at[it, d - 1], to, tm).wait_send()

        @pl.loop(0, blocks)
        def _(b):
            line = grad.at[it, half_rows(b, core), :]
            view = f_new.at[it, half_rows(b, core), :]
            remote(
                grad.at[it, half_rows(b, other), :], partner_in.at[it, slot_rows(b), :],
                pair_send.at[it, b], pair_recv.at[it, b], s, partner,
            ).wait_send()

            @pl.when(jnp.logical_not(is_owner))
            def _():
                remote(line, left_in.at[it, slot_rows(b), :], line_send.at[it, b], left_recv.at[it, b], s, tm).wait_send()

            @pl.when(both(has_left, chip <= owner))
            def _():
                remote(view, view, out_send.at[it, 0, b], gather_recv.at[it, b], s, tm).wait_send()

            @pl.when(both(has_right, chip >= owner))
            def _():
                remote(view, view, out_send.at[it, 1, b], gather_recv.at[it, b], s, tm).wait_send()

            remote(view, view, give_send.at[it, b], give_recv.at[it, b], s, partner).wait_send()

    x_store.wait()

    @pl.loop(0, blocks)
    def _(b):
        f_store(b).wait()


def solution(mesh):
    series_size, tm_size = mesh.shape["series"], mesh.shape["tm"]

    def local(observed, mask, series_factors, time_factors, ar_weights):
        rows, rank = series_factors.shape
        hours = time_factors.shape[1]
        blocks = rows // BLOCK
        piece = rank // series_size
        peers = max(series_size - 1, 1)
        f32, bf16 = jnp.float32, jnp.bfloat16
        vmem = pl.BlockSpec(memory_space=pltpu.VMEM)
        anywhere = pl.BlockSpec(memory_space=pl.ANY)
        dma = pltpu.SemaphoreType.DMA
        half = (ITERS, rows // 2, rank)
        f_last, x_last = pl.pallas_call(
            functools.partial(kernel, series_size, tm_size),
            out_shape=(
                jax.ShapeDtypeStruct((rows, rank), f32),
                jax.ShapeDtypeStruct((rank, hours), f32),
            ),
            in_specs=[anywhere, anywhere, vmem, vmem, vmem],
            out_specs=(anywhere, anywhere),
            scratch_shapes=[
                pltpu.VMEM((rows, hours), bf16),
                pltpu.VMEM((rows, hours), jnp.int32),
                pltpu.VMEM((ITERS, rows, rank), f32),
                pltpu.VMEM((ITERS, rank, hours), f32),
                pltpu.VMEM((rows, hours), bf16),
                pltpu.VMEM((rows, rank), bf16),
                pltpu.VMEM((rank, hours), bf16),
                pltpu.VMEM((ITERS, rows, rank), f32),
                pltpu.VMEM(half, f32),
                pltpu.VMEM(half, f32),
                pltpu.VMEM(half, f32),
                pltpu.VMEM((ITERS, rank, hours), f32),
                pltpu.VMEM((ITERS, peers, piece, hours), f32),
                pltpu.VMEM((ITERS, piece, HALO), f32),
                pltpu.VMEM((ITERS, piece, HALO), f32),
                pltpu.VMEM((3, rank, 128), f32),
                dma((2, blocks)),
                dma((blocks + 1,)),
                dma((ITERS, blocks)), dma((ITERS, blocks)),
                dma((ITERS, blocks)), dma((ITERS, blocks)), dma((ITERS, blocks)),
                dma((ITERS, 2, blocks)), dma((ITERS, blocks)),
                dma((ITERS, blocks)), dma((ITERS, blocks)),
                dma((ITERS, peers)), dma((ITERS, peers)),
                dma((ITERS, peers)), dma((ITERS, peers)),
                dma((ITERS, 2)), dma((ITERS, 2)),
            ],
            compiler_params=pltpu.CompilerParams(
                collective_id=0, has_side_effects=True, vmem_limit_bytes=60 * 1024 * 1024
            ),
        )(observed, mask, series_factors, time_factors, ar_weights)
        imputed = jnp.dot(
            f_last.astype(bf16), x_last.astype(bf16), preferred_element_type=f32
        ).astype(bf16)
        return f_last, x_last, imputed

    in_specs = (P("series", "tm"), P("series", "tm"), P("series", None), P(None, "tm"), P())
    out_specs = (P("series", None), P(None, "tm"), P("series", "tm"))
    return jax.shard_map(local, mesh=mesh, in_specs=in_specs, out_specs=out_specs, check_vma=False)
```

time: 151 us -> 77.1 us (0.51)
  waiting for transfers between devices: 99.6 us -> 0 us
  Pallas kernels: 0 us -> 70.2 us
  between operations: 15.4 us -> 0.65 us
  matrix products: 17 us -> 3.58 us
  other arithmetic: 9.74 us -> 0 us
  starting transfers between devices: 5.43 us -> 0 us
    pallas_call x0 -> x1, Pallas kernels: none -> 70.2 us  [local(): pl.pallas_call(functools.partial(kernel, series_size, tm_size), out_shape...]
    reduce_scatter x2 -> x0, waiting for transfers between devices: 62.5 us -> none  [local(): lax.psum_scatter(lax.dot_general(misfit, time_low, (((1,), (1,)), ((), ()...]
    psum x2 -> x0, waiting for transfers between devices: 22.1 us -> none  [local(): lax.psum(lax.dot_general(series_low, misfit, (((0,), (0,)), ((), ())), pr...]
    dot_general x7 -> x1, matrix products: 17 us -> 3.58 us  [local(): jnp.dot(f_last.astype(bf16), x_last.astype(bf16), preferred_element_type=...]
    all_gather x2 -> x0, waiting for transfers between devices: 8.86 us -> none  [local(): series_next = lax.all_gather(updated, 'tm', axis=0, tiled=True)]
    sub x4 -> x0, other arithmetic: 6.4 us -> none  [the longest x2 3.4 us: local(): updated = own_rows - step_f * (grad_share + ridge_f * own_rows)]
    ppermute x4 -> x0, waiting for transfers between devices: 5.98 us -> none  [passed_along(): return lax.ppermute(array, axis, pairs)]
    ppermute x4 -> x0, starting transfers between devices: 5.18 us -> none  [passed_along(): return lax.ppermute(array, axis, pairs)]
  transfers between devices with their start and end apart: 10 -> 0, of which waited for: 10 -> 0; matrix products, arithmetic and copies ran while one was open for 10% -> 0% of each run, Pallas kernels for 0% -> 0%
where the time goes in v1:
time: 77.1 us; the launch traced here: 76.9 us
  Pallas kernels  70.2 us (91%)
  matrix products  3.58 us (5%)
  local copies, waits for them, and re-layouts  2.49 us (3%)
    pallas_call x1, Pallas kernels, local(): pl.pallas_call(functools.partial(kernel, series_size, tm_size), out_shape...  70.2 us
    dot_general x1, matrix products, local(): jnp.dot(f_last.astype(bf16), x_last.astype(bf16), preferred_element_type=...  3.58 us
    unnamed x6, local copies, waits for them, and re-layouts  2.49 us

profile of v1, /device:TPU:0, one launch (start us, length us, event | category | flops | bytes accessed | tf_op | source)
XLA Modules:
  0.0 76.9 jit_solution(15218235486315578777)
XLA Ops:
  0.6 70.2 %shard_map.76 = (f32[1280,256]{1,0:T(8,128)}, f32[256,768]{1,0:T(8,128)}) custom-call(bf16[1280,768]{1,0:T(8,128)(2,1)} %obs_hbm.1, s32[1280,768]{1,0:T(8,128)} %mask_hbm.1, f32[1280,256]{1,0:T(8,128)} %f_in.1, f32[256,768]{1,0:T(8,128)} %x_in.1, f32[3,256]{1,0:T(4,128)} %w_in.1), custom_call_target="tpu_custom_call" | custom-call | tf_op jit(solution)/shard_map/pallas_call | solution.py:379
  70.8 0.0 copy-start
  70.8 3.6 %convolution_convert_fusion = bf16[1280,768]{1,0:T(8,128)(2,1)} fusion(f32[1280,256]{1,0:T(8,128)} %get-tuple-element.10, f32[256,768]{1,0:T(8,128)} %get-tuple-element.11), kind=kOutput, calls=%fused_computation | convolution fusion | flops 504823808 | bytes 4063232 | tf_op jit(solution)/shard_map/dot_general | solution.py:418
  74.4 0.0 copy-done
  74.4 0.0 copy-start.1
  74.4 1.1 %copy.10 = f32[1280,256]{1,0:T(8,128)} copy(f32[1280,256]{1,0:T(8,128)S(1)} %copy-done) | data formatting | bytes 2621440
  75.5 0.5 copy-done.1
  76.0 0.9 %copy.11 = f32[256,768]{1,0:T(8,128)} copy(f32[256,768]{1,0:T(8,128)S(1)} %copy-done.1) | data formatting | bytes 1572864
Async XLA Ops:
  70.8 3.6 %copy-start = (f32[1280,256]{1,0:T(8,128)S(1)}, f32[1280,256]{1,0:T(8,128)}, u32[]{:S(2)}) copy-start(f32[1280,256]{1,0:T(8,128)} %get-tuple-element.10) | copy-start | bytes 3932164
  74.4 1.6 %copy-start.1 = (f32[256,768]{1,0:T(8,128)S(1)}, f32[256,768]{1,0:T(8,128)}, u32[]{:S(2)}) copy-start(f32[256,768]{1,0:T(8,128)} %get-tuple-element.11) | copy-start | bytes 2359300

commit v2 on v1

--- a/solution.py
+++ b/solution.py
@@ -12,17 +12,21 @@
 HALO = 256
 HALF = 64
 BLOCK = 2 * HALF
+WIDE = 2
+TAIL_STEPS = 2
+PARTS = 2
 LAG_STEPS = 4
-G_STEP = 8
+EARLY = 0
+G_STEPS = ((5, 7), (5, 7))
 
 
 def kernel(
     series_size, tm_size,
-    obs_hbm, mask_hbm, f_in, x_in, w_in,
+    obs_hbm, mask_hbm, f_hbm, x_hbm, w_in,
     f_out, x_out,
-    obs, mask, f_new, x_new, misfit, f_low, x_low, grad, partner_in, left_in, right_in,
+    obs, mask, f_in, x_in, ar, f_new, x_new, misfit, f_low, x_low, grad, partner_in, left_in, right_in,
     g_loc, g_in, halo_l, halo_r, w_cols,
-    load_sem, out_sem, pair_send, pair_recv, line_send, left_recv, right_recv,
+    load_sem, first_sem, out_sem, pair_send, pair_recv, line_send, left_recv, right_recv,
     out_send, gather_recv, give_send, give_recv, g_send, g_recv, x_send, x_recv,
     edge_send, edge_recv,
 ):
@@ -80,10 +84,19 @@
             pltpu.make_async_copy(mask_hbm.at[block_rows(b), :], mask.at[block_rows(b), :], load_sem.at[1, b]),
         )
 
+    f_load = pltpu.make_async_copy(f_hbm, f_in, first_sem.at[0])
+    x_load = pltpu.make_async_copy(x_hbm, x_in, first_sem.at[1])
+    x_load.start()
+    f_load.start()
+
     @pl.loop(0, blocks)
     def _(b):
         for c in load_copies(b):
             c.start()
+
+    for lag in range(3):
+        w_cols[lag] = jnp.transpose(jnp.broadcast_to(w_in[lag : lag + 1, :], (128, rank)))
+    x_load.wait()
 
     barrier = pltpu.get_barrier_semaphore()
     for d in (-2, -1, 1, 2):
@@ -113,9 +126,10 @@
         pl.when(tm > 0)(to_left.start)
 
     start_edges(0, x_in)
-    for lag in range(3):
-        w_cols[lag] = jnp.transpose(jnp.broadcast_to(w_in[lag : lag + 1, :], (128, rank)))
-
+    f_load.wait()
+
+    spread_done = blocks + EARLY - LAG_STEPS
+    earlier_spread = None
     for it in range(ITERS):
         f_now = f_in if it == 0 else f_new.at[it - 1]
         x_now = x_in if it == 0 else x_new.at[it - 1]
@@ -161,55 +175,74 @@
 
         x_low[...] = x_now[...].astype(jnp.bfloat16)
 
-        def compute(b, carry):
-            if it == 0:
-                for c in load_copies(b):
-                    c.wait()
-            else:
-                give_wait(b, it - 1)
-            low = f_now[block_rows(b), :].astype(jnp.bfloat16)
-            f_low[block_rows(b), :] = low
+        def wide_rows(w):
+            return pl.ds(pl.multiple_of(w * WIDE * BLOCK, WIDE * BLOCK), WIDE * BLOCK)
+
+        def row_pass(w, carry, earlier_spread=earlier_spread):
+            for part in range(WIDE):
+                here = w * WIDE + part
+                if it == 0:
+                    for c in load_copies(here):
+                        c.wait()
+                else:
+                    pl.when(here >= spread_done)(lambda: earlier_spread(here))
+            if it > 0:
+                for part in range(WIDE):
+                    give_wait(w * WIDE + part, it - 1)
+            span = wide_rows(w)
+            low = f_now[span, :].astype(jnp.bfloat16)
+            f_low[span, :] = low
             product = jnp.dot(low, x_low[...], preferred_element_type=jnp.float32)
             miss = jnp.where(
-                mask[block_rows(b), :] != 0,
-                product - obs[block_rows(b), :].astype(jnp.float32),
+                mask[span, :] != 0,
+                product - obs[span, :].astype(jnp.float32),
                 jnp.zeros_like(product),
             ).astype(jnp.bfloat16)
-            misfit[block_rows(b), :] = miss
-            grad[it, block_rows(b), :] = lax.dot_general(
+            misfit[span, :] = miss
+            grad[it, span, :] = lax.dot_general(
                 miss, x_low[...], (((1,), (1,)), ((), ())), preferred_element_type=jnp.float32
             )
-            pair_copy(b).start()
-            pl.when(b > 0)(lambda: merge(b - 1))
+            for part in range(WIDE):
+                pair_copy(w * WIDE + part).start()
+
+            @pl.when(w > 0)
+            def _():
+                for part in range(WIDE):
+                    merge((w - 1) * WIDE + part)
+
             return carry
 
-        lax.fori_loop(0, blocks, compute, 0)
-        merge(blocks - 1)
-
-        g_loc[it] = lax.dot_general(
-            f_low[...], misfit[...], (((0,), (0,)), ((), ())), preferred_element_type=jnp.float32
-        )
-
-        def g_copy(d, it=it):
+        def columns(part):
+            return pl.ds(part * (hours // PARTS), hours // PARTS)
+
+        def g_copy(d, part, it=it):
             to = lax.rem(s + d, series_size)
             return remote(
-                g_loc.at[it, piece_rows(to), :], g_in.at[it, d - 1],
-                g_send.at[it, d - 1], g_recv.at[it, d - 1], to, tm,
-            )
-
-        def x_copy(d, it=it):
+                g_loc.at[it, piece_rows(to), columns(part)], g_in.at[it, d - 1, :, columns(part)],
+                g_send.at[it, part, d - 1], g_recv.at[it, part, d - 1], to, tm,
+            )
+
+        def x_copy(d, part, it=it):
             to = lax.rem(s + d, series_size)
-            view = x_new.at[it, piece_rows(s), :]
-            return remote(view, view, x_send.at[it, d - 1], x_recv.at[it, d - 1], to, tm)
-
-        def x_wait(d, it=it):
+            view = x_new.at[it, piece_rows(s), columns(part)]
+            return remote(view, view, x_send.at[it, part, d - 1], x_recv.at[it, part, d - 1], to, tm)
+
+        def x_wait(d, part, it=it):
             source = lax.rem(s + series_size - d, series_size)
-            view = x_new.at[it, piece_rows(source), :]
-            remote(view, view, x_send.at[it, d - 1], x_recv.at[it, d - 1], s, tm).wait_recv()
-
-        for d in range(1, series_size):
-            g_copy(d).start()
-
+            view = x_new.at[it, piece_rows(source), columns(part)]
+            remote(view, view, x_send.at[it, part, d - 1], x_recv.at[it, part, d - 1], s, tm).wait_recv()
+
+        wide = blocks // WIDE
+        lax.fori_loop(0, wide, row_pass, 0)
+        for part in range(WIDE):
+            merge((wide - 1) * WIDE + part)
+        for part in range(PARTS):
+            g_loc[it, :, columns(part)] = lax.dot_general(
+                f_low[...], misfit[:, columns(part)], (((0,), (0,)), ((), ())),
+                preferred_element_type=jnp.float32,
+            )
+            for d in range(1, series_size):
+                g_copy(d, part).start()
         def relay_step(b):
             @pl.when(both(relay, before))
             def _():
@@ -242,7 +275,7 @@
                 pl.when(has_right)(right.start)
                 give.start()
 
-        def spread_step(b):
+        def spread_step(b, spread_copies=spread_copies):
             left, right, give = spread_copies(b)
 
             @pl.when(jnp.logical_not(is_owner))
@@ -256,8 +289,6 @@
             pl.when(j < blocks)(lambda: relay_step(j))
             pl.when(j >= LAG_STEPS)(lambda: spread_step(j - LAG_STEPS))
             return carry
-
-        lax.fori_loop(0, G_STEP, line_step, 0)
 
         to_right, to_left = edge_copies(it, x_now)
 
@@ -290,21 +321,30 @@
         for lag in range(3):
             term = weights[lag] * pltpu.roll(resid, width - LAGS[lag], 1)
             back = term if back is None else back + term
-        ar = (resid - back)[:, HALO : HALO + hours]
-
-        total = g_loc[it, piece_rows(s), :]
-        for d in range(1, series_size):
-            g_copy(d).wait_recv()
-            total = total + g_in[it, d - 1]
-        x_new[it, piece_rows(s), :] = own - step_x * (total + ridge_x * own + lam_ar * ar)
-        for d in range(1, series_size):
-            x_copy(d).start()
+        ar[...] = (resid - back)[:, HALO : HALO + hours]
+
+        done = 0
+        for part in range(PARTS):
+            lax.fori_loop(done, G_STEPS[it][part], line_step, 0)
+            done = G_STEPS[it][part]
+            total = g_loc[it, piece_rows(s), columns(part)]
+            for d in range(1, series_size):
+                g_copy(d, part).wait_recv()
+                total = total + g_in[it, d - 1, :, columns(part)]
+            old = x_now[piece_rows(s), columns(part)]
+            x_new[it, piece_rows(s), columns(part)] = old - step_x * (
+                total + ridge_x * old + lam_ar * ar[:, columns(part)]
+            )
+            for d in range(1, series_size):
+                x_copy(d, part).start()
         if it < ITERS - 1:
             start_edges(it + 1, x_new.at[it])
 
-        lax.fori_loop(G_STEP, blocks + LAG_STEPS, line_step, 0)
-        for d in range(1, series_size):
-            x_wait(d)
+        lax.fori_loop(done, blocks + (LAG_STEPS if it == ITERS - 1 else EARLY), line_step, 0)
+        earlier_spread = spread_step
+        for part in range(PARTS):
+            for d in range(1, series_size):
+                x_wait(d, part)
 
     last = ITERS - 1
 
@@ -325,12 +365,14 @@
         pl.when(tm > 0)(to_left.wait_send)
         for d in range(1, series_size):
             to = lax.rem(s + d, series_size)
-            remote(
-                g_loc.at[it, piece_rows(to), :], g_in.at[it, d - 1],
-                g_send.at[it, d - 1], g_recv.at[it, d - 1], to, tm,
-            ).wait_send()
-            view = x_new.at[it, piece_rows(s), :]
-            remote(view, view, x_send.at[it, d - 1], x_recv.at[it, d - 1], to, tm).wait_send()
+            for part in range(PARTS):
+                span = pl.ds(part * (hours // PARTS), hours // PARTS)
+                remote(
+                    g_loc.at[it, piece_rows(to), span], g_in.at[it, d - 1, :, span],
+                    g_send.at[it, part, d - 1], g_recv.at[it, part, d - 1], to, tm,
+                ).wait_send()
+                view = x_new.at[it, piece_rows(s), span]
+                remote(view, view, x_send.at[it, part, d - 1], x_recv.at[it, part, d - 1], to, tm).wait_send()
 
         @pl.loop(0, blocks)
         def _(b):
@@ -360,6 +402,18 @@
     @pl.loop(0, blocks)
     def _(b):
         f_store(b).wait()
+
+
+def final_product(f_ref, x_ref, f_out, x_out, imputed, x_low):
+    @pl.when(pl.program_id(0) == 0)
+    def _():
+        x_out[...] = x_ref[...]
+        x_low[...] = x_ref[...].astype(jnp.bfloat16)
+
+    f_out[...] = f_ref[...]
+    imputed[...] = jnp.dot(
+        f_ref[...].astype(jnp.bfloat16), x_low[...], preferred_element_type=jnp.float32
+    ).astype(jnp.bfloat16)
 
 
 def solution(mesh):
@@ -382,11 +436,14 @@
                 jax.ShapeDtypeStruct((rows, rank), f32),
                 jax.ShapeDtypeStruct((rank, hours), f32),
             ),
-            in_specs=[anywhere, anywhere, vmem, vmem, vmem],
+            in_specs=[anywhere, anywhere, anywhere, anywhere, vmem],
             out_specs=(anywhere, anywhere),
             scratch_shapes=[
                 pltpu.VMEM((rows, hours), bf16),
                 pltpu.VMEM((rows, hours), jnp.int32),
+                pltpu.VMEM((rows, rank), f32),
+                pltpu.VMEM((rank, hours), f32),
+                pltpu.VMEM((piece, hours), f32),
                 pltpu.VMEM((ITERS, rows, rank), f32),
                 pltpu.VMEM((ITERS, rank, hours), f32),
                 pltpu.VMEM((rows, hours), bf16),
@@ -402,23 +459,35 @@
                 pltpu.VMEM((ITERS, piece, HALO), f32),
                 pltpu.VMEM((3, rank, 128), f32),
                 dma((2, blocks)),
+                dma((2,)),
                 dma((blocks + 1,)),
                 dma((ITERS, blocks)), dma((ITERS, blocks)),
                 dma((ITERS, blocks)), dma((ITERS, blocks)), dma((ITERS, blocks)),
                 dma((ITERS, 2, blocks)), dma((ITERS, blocks)),
                 dma((ITERS, blocks)), dma((ITERS, blocks)),
-                dma((ITERS, peers)), dma((ITERS, peers)),
-                dma((ITERS, peers)), dma((ITERS, peers)),
+                dma((ITERS, PARTS, peers)), dma((ITERS, PARTS, peers)),
+                dma((ITERS, PARTS, peers)), dma((ITERS, PARTS, peers)),
                 dma((ITERS, 2)), dma((ITERS, 2)),
             ],
             compiler_params=pltpu.CompilerParams(
                 collective_id=0, has_side_effects=True, vmem_limit_bytes=60 * 1024 * 1024
             ),
         )(observed, mask, series_factors, time_factors, ar_weights)
-        imputed = jnp.dot(
-            f_last.astype(bf16), x_last.astype(bf16), preferred_element_type=f32
-        ).astype(bf16)
-        return f_last, x_last, imputed
+        tall = rows // TAIL_STEPS
+        by_row = lambda width: pl.BlockSpec((tall, width), lambda i: (i, 0))
+        whole = pl.BlockSpec((rank, hours), lambda i: (0, 0))
+        return tuple(pl.pallas_call(
+            final_product,
+            grid=(TAIL_STEPS,),
+            out_shape=(
+                jax.ShapeDtypeStruct((rows, rank), f32),
+                jax.ShapeDtypeStruct((rank, hours), f32),
+                jax.ShapeDtypeStruct((rows, hours), bf16),
+            ),
+            in_specs=[by_row(rank), whole],
+            out_specs=(by_row(rank), whole, by_row(hours)),
+            scratch_shapes=[pltpu.VMEM((rank, hours), bf16)],
+        )(f_last, x_last))
 
     in_specs = (P("series", "tm"), P("series", "tm"), P("series", None), P(None, "tm"), P())
     out_specs = (P("series", None), P(None, "tm"), P("series", "tm"))

time: 77.1 us -> 68.3 us (0.89)
  matrix products: 3.58 us -> 0 us
  Pallas kernels: 70.2 us -> 67.4 us
  local copies, waits for them, and re-layouts: 2.49 us -> 0 us
    pallas_call x1, Pallas kernels: 70.2 us -> 63.6 us  [local(): pl.pallas_call(functools.partial(kernel, series_size, tm_size), out_shape...]
    pallas_call x0 -> x1, Pallas kernels: none -> 3.78 us  [local(): pl.pallas_call(final_product, grid=(TAIL_STEPS,), out_shape=(jax.ShapeDty...]
    dot_general x1 -> x0, matrix products: 3.58 us -> none  [local(): jnp.dot(f_last.astype(bf16), x_last.astype(bf16), preferred_element_type=...]
    unnamed x6 -> x0, local copies, waits for them, and re-layouts: 2.49 us -> none
where the time goes in v2:
time: 68.3 us; the launch traced here: 68.1 us
  Pallas kernels  67.4 us (99%)
    pallas_call x1, Pallas kernels, local(): pl.pallas_call(functools.partial(kernel, series_size, tm_size), out_shape...  63.6 us
    pallas_call x1, Pallas kernels, local(): pl.pallas_call(final_product, grid=(TAIL_STEPS,), out_shape=(jax.ShapeDty...  3.78 us

profile of v2, /device:TPU:0, one launch (start us, length us, event | category | flops | bytes accessed | tf_op | source)
XLA Modules:
  0.0 68.1 jit_solution(781288708208261077)
XLA Ops:
  0.6 63.6 %shard_map.76 = (f32[1280,256]{1,0:T(8,128)}, f32[256,768]{1,0:T(8,128)}) custom-call(bf16[1280,768]{1,0:T(8,128)(2,1)} %obs_hbm.1, s32[1280,768]{1,0:T(8,128)} %mask_hbm.1, f32[1280,256]{1,0:T(8,128)} %f_hbm.1, f32[256,768]{1,0:T(8,128)} %x_hbm.1, f32[3,256]{1,0:T(4,128)} %w_in.1), custom_call_target="tpu_custom_call" | custom-call | tf_op jit(solution)/shard_map/pallas_call | solution.py:433
  64.3 3.8 %shard_map.77 = (f32[1280,256]{1,0:T(8,128)}, f32[256,768]{1,0:T(8,128)}, bf16[1280,768]{1,0:T(8,128)(2,1)}) custom-call(f32[1280,256]{1,0:T(8,128)} %get-tuple-element.5.f_ref, f32[256,768]{1,0:T(8,128)} %get-tuple-element.6.x_ref), custom_call_target="tpu_custom_call" | custom-call | tf_op jit(solution)/shard_map/pallas_call | solution.py:479
